TPU v7x, 256 devices: a whole 4x4x8 slice. The times are simulated.
256 devices in a mesh: lon: 64 (over x_hi, z, y), lat: 4 (over x_lo, core).
Axes of the slice: x: 4 (x_hi: 2, x_lo: 2; x = x_hi * 2 + x_lo), y: 4, z: 8, core: 2. Of those that a mesh axis runs over, the one named last changes fastest.
Arguments:
- height: float32 [256, 16000], P('lat', 'lon'), may hold values from -6 to 6
- divergence: float32 [256, 16000], P('lat', 'lon'), may hold values from -6 to 6
- depth: float32 [256, 16000], P('lat', 'lon'), may hold values from 0.25 to 4
- tide: float32 [256, 16000], P('lat', 'lon'), may hold values from -6 to 6
- gauss_weight: float32 [128], P('lat'), may hold values from 0.5 to 1.5
- legendre: bfloat16 [1792, 128, 3585], P('lon', 'lat'), may hold values from -4 to 4
Outputs:
- height_new: float32 [256, 16000], P('lat', 'lon')
- divergence_new: float32 [256, 16000], P('lat', 'lon')
All inputs are finite; a program needn't handle non-finite values.
Results may differ from a plain program's by a relative error of at most 0.0032.
Values may be sent and summed in bfloat16 or wider, within the bound.
A program may use at most 128 MiB of HBM per device.

v0:
```python
import math
import jax
import jax.numpy as jnp
from jax import lax
from jax.sharding import PartitionSpec as P

time_step = 0.5
drag_step = 0.1
coupling = 2.0
gravity_step = 4.0
section_length = 128
highest = lax.Precision.HIGHEST


def angle_table(first_index, second, period):
    product = first_index[:, None] * second[None, :] % period
    angle_value = product.astype(jnp.float32) * (2.0 * math.pi / period)
    return (jnp.cos(angle_value), jnp.sin(angle_value))


def slot_layout(pair_first, pair_count, wave_count, slot_count):
    pair_index = pair_first + jnp.arange(pair_count, dtype=jnp.int32)
    slot_index = jnp.arange(slot_count, dtype=jnp.int32)[None, :]
    pair_column = pair_index[:, None]
    upper_slot = slot_index >= wave_count - pair_column
    degree = jnp.where(upper_slot, slot_index - 1, pair_column + slot_index)
    parity = jnp.where(upper_slot, (slot_index + pair_column + wave_count) % 2, slot_index % 2)
    eigen_value = (
        degree.astype(jnp.float32)
        * (degree + 1).astype(jnp.float32)
        / float(wave_count * wave_count)
    )
    return (upper_slot, parity, eigen_value)


def helmholtz(height_rhs, div_rhs, eigen_value):
    height_spec = (height_rhs - time_step * div_rhs) / (1.0 + coupling * eigen_value)
    div_spec = div_rhs + gravity_step * eigen_value * height_spec
    return jnp.stack([height_spec, div_spec]).astype(jnp.bfloat16)


def forward_fourier(row_block, wave_count, lon_groups):
    item_count, row_count, lon_total = row_block.shape
    inner_count = lon_total // section_length
    outer_count = -(-wave_count // section_length)
    flat_rows = row_block.reshape(item_count * row_count, section_length, inner_count)
    section_index = jnp.arange(section_length, dtype=jnp.int32)
    inner_index = jnp.arange(inner_count, dtype=jnp.int32)
    outer_index = jnp.arange(outer_count, dtype=jnp.int32)
    first_cos, first_sin = angle_table(section_index, section_index, section_length)
    section_real = jnp.einsum("qab,ak->qkb", flat_rows, first_cos, precision=highest)
    section_imag = -jnp.einsum("qab,ak->qkb", flat_rows, first_sin, precision=highest)
    twist_cos, twist_sin = angle_table(section_index, inner_index, lon_total)
    turned_real = section_real * twist_cos + section_imag * twist_sin
    turned_imag = section_imag * twist_cos - section_real * twist_sin
    second_cos, second_sin = angle_table(inner_index, outer_index, inner_count)
    wave_real = jnp.einsum("qkb,bt->qtk", turned_real, second_cos, precision=highest) + jnp.einsum(
        "qkb,bt->qtk", turned_imag, second_sin, precision=highest
    )
    wave_imag = jnp.einsum("qkb,bt->qtk", turned_imag, second_cos, precision=highest) - jnp.einsum(
        "qkb,bt->qtk", turned_real, second_sin, precision=highest
    )
    lon_scale = 1.0 / lon_total
    wave_real = wave_real.reshape(item_count * row_count, outer_count * section_length) * lon_scale
    wave_imag = wave_imag.reshape(item_count * row_count, outer_count * section_length) * lon_scale
    half_count = wave_count // 2
    pair_count = half_count // lon_groups

    def arrange(values):
        lower_part = values[:, :half_count].reshape(-1, lon_groups, pair_count)
        upper_part = values[:, half_count:][:, ::-1].reshape(-1, lon_groups, pair_count)
        return jnp.stack([lower_part, upper_part], axis=2)

    packed = jnp.stack([arrange(wave_real), arrange(wave_imag)], axis=2)
    return packed.reshape(item_count, row_count, lon_groups * 4 * pair_count)


def inverse_fourier(packed, wave_count, lon_groups, lon_total):
    item_count, row_count, width_count = packed.shape
    half_count = wave_count // 2
    pair_count = half_count // lon_groups
    split_form = packed.reshape(item_count * row_count, lon_groups, 2, 2, pair_count)
    lower_part = jnp.transpose(split_form[:, :, :, 0], (0, 2, 1, 3)).reshape(-1, 2, half_count)
    upper_part = jnp.transpose(split_form[:, :, :, 1], (0, 2, 1, 3)).reshape(-1, 2, half_count)[
        :, :, ::-1
    ]
    ordered = jnp.concatenate([lower_part, upper_part], axis=2)
    wave_index = jnp.arange(wave_count, dtype=jnp.int32)
    factor = jnp.where(wave_index == 0, 1.0, 2.0).astype(jnp.float32)
    inner_count = lon_total // section_length
    outer_count = -(-wave_count // section_length)
    coef_real = (ordered[:, 0] * factor).reshape(-1, outer_count, section_length)
    coef_imag = (ordered[:, 1] * factor).reshape(-1, outer_count, section_length)
    section_index = jnp.arange(section_length, dtype=jnp.int32)
    inner_index = jnp.arange(inner_count, dtype=jnp.int32)
    outer_index = jnp.arange(outer_count, dtype=jnp.int32)
    second_cos, second_sin = angle_table(outer_index, inner_index, inner_count)
    part_real = jnp.einsum("qtk,tb->qkb", coef_real, second_cos, precision=highest) - jnp.einsum(
        "qtk,tb->qkb", coef_imag, second_sin, precision=highest
    )
    part_imag = jnp.einsum("qtk,tb->qkb", coef_real, second_sin, precision=highest) + jnp.einsum(
        "qtk,tb->qkb", coef_imag, second_cos, precision=highest
    )
    twist_cos, twist_sin = angle_table(section_index, inner_index, lon_total)
    turned_real = part_real * twist_cos - part_imag * twist_sin
    turned_imag = part_real * twist_sin + part_imag * twist_cos
    first_cos, first_sin = angle_table(section_index, section_index, section_length)
    grid_rows = jnp.einsum("qkb,ak->qab", turned_real, first_cos, precision=highest) - jnp.einsum(
        "qkb,ak->qab", turned_imag, first_sin, precision=highest
    )
    return grid_rows.reshape(item_count, row_count, lon_total)


def per_device(height, divergence, depth, tide, gauss_weight, legendre):
    lon_groups = lax.axis_size("lon")
    lat_groups = lax.axis_size("lat")
    pair_count, north_count, slot_count = legendre.shape
    wave_count = 2 * pair_count * lon_groups
    lat_count = 2 * north_count * lat_groups
    lon_total = height.shape[1] * lon_groups
    norm_factor = math.sqrt(lon_total / lat_count) / wave_count
    forcing = jnp.stack(
        [
            height - time_step * (depth - 1.0) * divergence,
            divergence * (1.0 - drag_step / depth),
            tide,
        ]
    )
    spread = forward_fourier(
        lax.all_to_all(forcing, "lon", split_axis=1, concat_axis=2, tiled=True),
        wave_count,
        lon_groups,
    )
    band_waves = lax.all_to_all(spread, "lon", split_axis=2, concat_axis=1, tiled=True)
    band_form = band_waves.reshape(3, 2, north_count, 2, 2, pair_count)
    weight = (gauss_weight * norm_factor)[None, :, None, None, None]
    even_part = (band_form[:, 0] + band_form[:, 1]) * weight
    odd_part = (band_form[:, 0] - band_form[:, 1]) * weight
    folded = jnp.stack([even_part, odd_part], axis=1).astype(jnp.bfloat16)
    lat_sums = jnp.einsum(
        "ijk,fqjrai->afqrik", legendre, folded, preferred_element_type=jnp.float32
    )
    upper_slot, parity, eigen_value = slot_layout(
        lax.axis_index("lon") * pair_count, pair_count, wave_count, slot_count
    )
    odd_slot = parity == 1
    lower_slot = jnp.logical_not(upper_slot)
    even_slot = jnp.logical_not(odd_slot)
    select_masks = jnp.stack(
        [
            jnp.stack([lower_slot & even_slot, lower_slot & odd_slot]),
            jnp.stack([upper_slot & even_slot, upper_slot & odd_slot]),
        ]
    ).astype(jnp.float32)
    spectral = jnp.einsum("aqik,afqrik->frik", select_masks, lat_sums, precision=highest)
    summed = lax.psum(spectral, "lat")
    div_rhs = summed[1] - gravity_step * eigen_value * summed[2]
    solved = helmholtz(summed[0], div_rhs, eigen_value)
    member_masks = jnp.stack([lower_slot, upper_slot]).astype(jnp.bfloat16)
    parity_masks = jnp.stack([even_slot, odd_slot]).astype(jnp.bfloat16)
    masked = (
        solved[None, None] * member_masks[:, None, None, None] * parity_masks[None, :, None, None]
    )
    slot_sums = jnp.einsum(
        "ijk,aqfrik->fqjrai", legendre, masked, preferred_element_type=jnp.float32
    )
    north_part = slot_sums[:, 0] + slot_sums[:, 1]
    south_part = slot_sums[:, 0] - slot_sums[:, 1]
    grid_waves = jnp.stack([north_part, south_part], axis=1).reshape(
        2, 2 * north_count, 4 * pair_count
    )
    lon_rows = inverse_fourier(
        lax.all_to_all(grid_waves, "lon", split_axis=1, concat_axis=2, tiled=True),
        wave_count,
        lon_groups,
        lon_total,
    )
    new_fields = lax.all_to_all(lon_rows, "lon", split_axis=2, concat_axis=1, tiled=True)
    return (new_fields[0], new_fields[1])


def solution(mesh):
    in_specs = (
        P("lat", "lon"),
        P("lat", "lon"),
        P("lat", "lon"),
        P("lat", "lon"),
        P("lat"),
        P("lon", "lat", None),
    )
    out_specs = (P("lat", "lon"), P("lat", "lon"))
    return jax.shard_map(
        per_device, mesh=mesh, in_specs=in_specs, out_specs=out_specs, check_vma=False
    )
```

profile of v0, /device:TPU:8, one launch (start us, length us, event | category | flops | bytes accessed | tf_op | source)
XLA Modules:
  0.0 645.9 jit_solution(13168154059006172092)
XLA Ops:
  7.2 0.9 stack.74
  8.1 0.9 multiply_subtract_fusion.1
  9.1 0.9 pad_maximum_fusion.1
  10.0 14.6 %all-to-all-start = ((f32[3,64,250]{2,0,1:T(4,128)}), f32[3,64,250]{2,0,1:T(4,128)S(1)}, u32[]{:S(2)}, u32[]{:S(2)}) async-start(f32[3,64,250]{2,0,1:T(4,128)} %pad_maximum_fusion.1), calls=%async_computation | async-start | bytes 524288 | tf_op jit(solution)/shard_map/all_to_all | solution.py:130
  24.6 2.9 not_and_fusion.1
  27.5 3.0 not_and_fusion.2
  30.5 1.0 add_bitcast_fusion.1
  31.5 1.0 add_bitcast_fusion.2
  32.5 0.9 fusion.5
  33.4 0.9 copy.91
  34.2 0.3 fusion.56
  34.5 3.9 all-to-all-done
  38.5 0.6 convolution_negate_fusion
  39.1 0.6 fusion.47
  39.8 0.4 fusion.24
  40.2 0.4 fusion.28
  40.6 0.4 fusion.15
  41.1 1.2 rev.10
  42.4 0.4 fusion.17
  42.9 1.2 rev.9
  45.4 0.3 copy.64
  45.7 0.6 reshape.830
  46.3 5.7 copy.65
  51.9 0.5 broadcast.873
  52.5 34.1 %reduce.10 = f32[7168,3]{1,0:T(8,128)} reduce(f32[7168,1,3]{2,1,0:T(1,128)} %bitcast.112, f32[]{:T(128)} %broadcast.873), dimensions={1}, to_apply=%bitcast.101.reduce_sub_computation | reduce | bytes 172036
  86.5 4.3 reshape.853
  90.8 8.9 %all-to-all-start.1 = ((f32[64,1,336]{2,1,0:T(1,128)}), f32[64,1,336]{2,1,0:T(1,128)S(1)}, u32[]{:S(2)}, u32[]{:S(2)}) async-start(f32[64,1,336]{2,1,0:T(1,128)} %reshape.853), calls=%async_computation.1 | async-start | bytes 196608 | tf_op jit(solution)/shard_map/all_to_all | solution.py:134
  99.8 11.4 %all-to-all-done.1 = f32[64,1,336]{2,1,0:T(1,128)S(1)} async-done(((f32[64,1,336]{2,1,0:T(1,128)}), f32[64,1,336]{2,1,0:T(1,128)S(1)}, u32[]{:S(2)}, u32[]{:S(2)}) %all-to-all-start.1) | async-done | bytes 86048 | tf_op jit(solution)/shard_map/all_to_all | solution.py:134
  111.3 0.9 reduce.11
  112.1 6.9 %reshape.854 = f32[7168,1,3]{2,1,0:T(1,128)} reshape(f32[64,336]{1,0:T(8,128)S(1)} %reduce.11) | data formatting | bytes 172032
  119.0 7.1 %copy.66 = f32[3,1,7168]{2,0,1:T(4,128)S(1)} copy(f32[3,1,7168]{0,1,2:T(1,128)} %bitcast.111) | data formatting | bytes 172032 | tf_op jit(solution)/shard_map/all_to_all | solution.py:134
  126.1 0.7 reshape.831
  127.5 19.9 %fusion = f32[28,3585,3,2]{1,3,2,0:T(2,128)} fusion(bf16[28,32,3585]{2,1,0:T(8,128)(2,1)} %param.11, f32[28,3585,2,2]{1,2,3,0:T(2,128)S(1)} %copy.91, bf16[3,1,32,2,2,28]{2,4,3,1,0,5:T(2,128)(2,1)S(1)} %get-tuple-element.17, bf16[3,1,32,2,2,28]{2,4,3,1,0,5:T(2,128)(2,1)S(1)} %get-tuple-element.16), kind=kOutput, calls=%fused_computation.1 | convolution fusion | flops 158485664 | bytes 10482528 | tf_op jit(solution)/shard_map/ijk,fqjrai->afqrik/dot_general | solution.py:140
  147.4 2.0 add_convert_fusion.1
  149.4 1.0 add_convert_fusion
  150.4 0.2 fusion.20
  150.7 59.3 %all-reduce.2.cloned.1.call-done = f32[3,2,28,3585]{3,1,0,2:T(2,128)} async-done(((f32[3,2,28,3585]{3,1,0,2:T(2,128)}), f32[3,2,28,3585]{3,1,0,2:T(2,128)}) %all-reduce.2.cloned.1.call-update) | async-done | bytes 2409136 | tf_op jit(solution)/shard_map/psum | solution.py:156
  210.0 2.7 fusion.182
  212.6 0.8 add_convert_fusion.2
  213.4 1.1 pad_maximum_fusion
  214.6 1.8 broadcast_multiply_fusion
  216.4 7.6 %fusion.8 = f32[2,2,32,2,2,28]{2,3,0,1,4,5:T(2,128)S(1)} fusion(bf16[28,32,3585]{2,1,0:T(8,128)(2,1)} %param.11, bf16[2,28,3585]{2,0,1:T(2,128)(2,1)S(1)} %add_convert_fusion.1, bf16[2,2,2,28,3585]{4,2,1,0,3:T(2,128)(2,1)S(1)} %broadcast_multiply_fusion), kind=kOutput, calls=%fused_computation.19 | convolution fusion | flops 109213440 | bytes 8489264 | tf_op jit(solution)/shard_map/ijk,aqfrik->fqjrai/dot_general | solution.py:164
  224.2 0.3 copy.87
  224.5 0.9 reshape.848
  225.4 12.8 %all-to-all-start.2 = ((f32[2,64,112]{2,0,1:T(2,128)}), f32[2,64,112]{2,0,1:T(2,128)S(1)}, u32[]{:S(2)}, u32[]{:S(2)}) async-start(f32[2,64,112]{2,0,1:T(2,128)} %reshape.848), calls=%async_computation.2 | async-start | bytes 131072 | tf_op jit(solution)/shard_map/all_to_all | solution.py:173
  238.3 11.3 %all-to-all-done.2 = f32[2,64,112]{2,0,1:T(2,128)S(1)} async-done(((f32[2,64,112]{2,0,1:T(2,128)}), f32[2,64,112]{2,0,1:T(2,128)S(1)}, u32[]{:S(2)}, u32[]{:S(2)}) %all-to-all-start.2) | async-done | bytes 57376 | tf_op jit(solution)/shard_map/all_to_all | solution.py:173
  250.2 1.3 rev.11
  251.4 0.2 fusion.75
  251.7 0.4 fusion.70
  252.1 0.4 fusion.72
  252.5 0.4 convolution_add_fusion
  252.9 0.4 convolution_subtract_fusion.1
  253.3 0.5 fusion.36
  253.9 0.5 fusion.13
  254.4 0.3 reshape.836
  254.7 11.8 %copy.74 = f32[2,1,16000]{0,1,2:T(1,128)} copy(f32[2,1,16000]{2,0,1:T(2,128)S(1)} %reshape.836) | data formatting | bytes 256000 | tf_op jit(solution)/shard_map/reshape | solution.py:111
  266.5 72.8 %reduce.12 = f32[16000,2]{1,0:T(8,128)} reduce(f32[16000,1,2]{2,1,0:T(1,128)} %bitcast.110, f32[]{:T(128)} %broadcast.873), dimensions={1}, to_apply=%bitcast.103.reduce_sub_computation | reduce | bytes 256004
  339.3 6.7 %reshape.855 = f32[64,1,500]{2,1,0:T(1,128)S(1)} reshape(f32[16000,2]{1,0:T(8,128)} %reduce.12) | data formatting | bytes 256000
  346.0 16.7 %all_to_all.16 = f32[64,1,500]{2,1,0:T(1,128)S(1)} all-to-all(f32[64,1,500]{2,1,0:T(1,128)S(1)} %reshape.855), channel_id=1, replica_groups=mesh['lon'=64,'lat'=4] {'lon'}, dimensions={0} | all-to-all | bytes 256000 | tf_op jit(solution)/shard_map/all_to_all | solution.py:178
  362.7 1.0 reduce.13
  363.6 10.4 %reshape.856 = f32[16000,1,2]{2,1,0:T(1,128)} reshape(f32[64,500]{1,0:T(8,128)S(1)} %reduce.13) | data formatting | bytes 256000
  374.1 263.0 %slice_reduce_fusion = (f32[16000]{0:T(1024)S(1)}, f32[16000]{0:T(1024)S(1)}) fusion(f32[2,1,16000]{0,1,2:T(1,128)} %bitcast.109), kind=kLoop, calls=%fused_computation.2 | loop fusion | bytes 256000 | tf_op jit(solution)/shard_map/slice | solution.py:179
  637.0 0.8 squeeze.34
  637.9 0.8 squeeze.16
  (46 shorter events, 3.2 us)
Async XLA Ops:
  10.0 28.4 %all-to-all-start = ((f32[3,64,250]{2,0,1:T(4,128)}), f32[3,64,250]{2,0,1:T(4,128)S(1)}, u32[]{:S(2)}, u32[]{:S(2)}) async-start(f32[3,64,250]{2,0,1:T(4,128)} %pad_maximum_fusion.1), calls=%async_computation | async-start | bytes 524288 | tf_op jit(solution)/shard_map/all_to_all | solution.py:130
  86.5 13.3 %copy-start.2 = (f32[32]{0:T(128)S(1)}, f32[32]{0:T(128)}, u32[]{:S(2)}) copy-start(f32[32]{0:T(128)} %param.10) | copy-start | bytes 388
  90.8 20.4 %all-to-all-start.1 = ((f32[64,1,336]{2,1,0:T(1,128)}), f32[64,1,336]{2,1,0:T(1,128)S(1)}, u32[]{:S(2)}, u32[]{:S(2)}) async-start(f32[64,1,336]{2,1,0:T(1,128)} %reshape.853), calls=%async_computation.1 | async-start | bytes 196608 | tf_op jit(solution)/shard_map/all_to_all | solution.py:134
  99.8 110.2 %all-reduce.2.cloned.1.call-start = ((), (), s32[]{:S(2)}) async-start(), calls=%async_computation.4 | async-start | bytes 4988928 | tf_op jit(solution)/shard_map/psum | solution.py:156
  147.4 2.1 copy-start.1
  209.9 2.7 copy-start
  225.4 24.1 %all-to-all-start.2 = ((f32[2,64,112]{2,0,1:T(2,128)}), f32[2,64,112]{2,0,1:T(2,128)S(1)}, u32[]{:S(2)}, u32[]{:S(2)}) async-start(f32[2,64,112]{2,0,1:T(2,128)} %reshape.848), calls=%async_computation.2 | async-start | bytes 131072 | tf_op jit(solution)/shard_map/all_to_all | solution.py:173
Sparse Core Ops, SparseCore 0:
  147.5 62.3 all-reduce.1
where the time goes:
time: 656 us; the launch traced here: 646 us
  local copies, waits for them, and re-layouts  329 us (50%)
  other arithmetic  130 us (20%)
  waiting for transfers between devices  85.8 us (13%)
  starting transfers between devices  36.4 us (6%)
  matrix products  33.1 us (5%)
  blocking collectives  16.7 us (3%)
  between operations  14.9 us (2%)
    slice x1, local copies, waits for them, and re-layouts, per_device(): return (new_fields[0], new_fields[1])  263 us
    unnamed x3, other arithmetic  108 us
    psum x1, waiting for transfers between devices, per_device(): summed = lax.psum(spectral, 'lat')  59.3 us
    unnamed x16, local copies, waits for them, and re-layouts  30.1 us
    dot_general x1, matrix products, per_device(): jnp.einsum('ijk,fqjrai->afqrik', legendre, folded, preferred_element_type...  19.9 us
    all_to_all x1, blocking collectives, per_device(): lax.all_to_all(lon_rows, 'lon', split_axis=2, concat_axis=1, tiled=True)  16.7 us
    all_to_all x1, starting transfers between devices, per_device(): lax.all_to_all(forcing, 'lon', split_axis=1, concat_axis=2, tiled=True)  14.6 us
  transfers between devices with their start and end apart: 4, of which 4 were waited for; matrix products, arithmetic and copies ran while one was open for 2% of the time, Pallas kernels for 0%

commit v1 on v0

--- a/solution.py
+++ b/solution.py
@@ -153,7 +153,7 @@
         ]
     ).astype(jnp.float32)
     spectral = jnp.einsum("aqik,afqrik->frik", select_masks, lat_sums, precision=highest)
-    summed = lax.psum(spectral, "lat")
+    summed = jnp.sum(lax.all_gather(spectral, "lat"), 0)
     div_rhs = summed[1] - gravity_step * eigen_value * summed[2]
     solved = helmholtz(summed[0], div_rhs, eigen_value)
     member_masks = jnp.stack([lower_slot, upper_slot]).astype(jnp.bfloat16)

time: 656 us -> 701 us (1.069)
  waiting for transfers between devices: 85.8 us -> 111 us
  other arithmetic: 130 us -> 145 us
    all_gather x0 -> x1, waiting for transfers between devices: none -> 84.5 us  [per_device(): summed = jnp.sum(lax.all_gather(spectral, 'lat'), 0)]
    psum x1 -> x0, waiting for transfers between devices: 59.3 us -> none  [per_device(): summed = lax.psum(spectral, 'lat')]
    reduce_sum x0 -> x1, other arithmetic: none -> 13.5 us  [per_device(): summed = jnp.sum(lax.all_gather(spectral, 'lat'), 0)]
    unnamed x16 -> x20, local copies, waits for them, and re-layouts: 30.1 us -> 30.1 us
where the time goes in v1:
time: 701 us; the launch traced here: 690 us
  local copies, waits for them, and re-layouts  333 us (48%)
  other arithmetic  145 us (21%)
  waiting for transfers between devices  111 us (16%)
  starting transfers between devices  36.6 us (5%)
  matrix products  33.1 us (5%)
  blocking collectives  17.2 us (2%)
  between operations  15 us (2%)
    slice x1, local copies, waits for them, and re-layouts, per_device(): return (new_fields[0], new_fields[1])  263 us
    unnamed x3, other arithmetic  108 us
    all_gather x1, waiting for transfers between devices, per_device(): summed = jnp.sum(lax.all_gather(spectral, 'lat'), 0)  84.5 us
    unnamed x20, local copies, waits for them, and re-layouts  30.1 us
    dot_general x1, matrix products, per_device(): jnp.einsum('ijk,fqjrai->afqrik', legendre, folded, preferred_element_type...  19.9 us
    all_to_all x1, blocking collectives, per_device(): lax.all_to_all(lon_rows, 'lon', split_axis=2, concat_axis=1, tiled=True)  17.2 us
    all_to_all x1, starting transfers between devices, per_device(): lax.all_to_all(forcing, 'lon', split_axis=1, concat_axis=2, tiled=True)  14.6 us
  transfers between devices with their start and end apart: 4, of which 4 were waited for; matrix products, arithmetic and copies ran while one was open for 2% of the time, Pallas kernels for 0%

profile of v1, /device:TPU:8, one launch (start us, length us, event | category | flops | bytes accessed | tf_op | source)
XLA Modules:
  0.0 690.4 jit_solution(5797792519826307311)
XLA Ops:
  7.2 0.9 stack.74
  8.1 0.9 multiply_subtract_fusion.1
  9.1 0.9 pad_maximum_fusion.1
  10.0 14.6 %all-to-all-start = ((f32[3,64,250]{2,0,1:T(4,128)}), f32[3,64,250]{2,0,1:T(4,128)S(1)}, u32[]{:S(2)}, u32[]{:S(2)}) async-start(f32[3,64,250]{2,0,1:T(4,128)} %pad_maximum_fusion.1), calls=%async_computation | async-start | bytes 524288 | tf_op jit(solution)/shard_map/all_to_all | solution.py:130
  24.6 2.9 not_and_fusion.1
  27.5 3.1 not_and_fusion.2
  30.5 1.0 add_bitcast_fusion.1
  31.5 1.0 add_bitcast_fusion.2
  32.5 0.9 fusion.5
  33.4 0.9 copy.95
  34.3 0.3 fusion.56
  34.5 3.9 all-to-all-done
  38.5 0.6 convolution_negate_fusion
  39.1 0.6 fusion.47
  39.8 0.4 fusion.24
  40.2 0.4 fusion.28
  40.6 0.4 fusion.15
  41.1 1.2 rev.10
  42.4 0.4 fusion.17
  42.8 1.2 rev.9
  45.4 0.3 copy.66
  45.7 0.6 reshape.830
  46.3 5.7 copy.67
  51.9 0.5 broadcast.873
  52.4 34.1 %reduce.10 = f32[7168,3]{1,0:T(8,128)} reduce(f32[7168,1,3]{2,1,0:T(1,128)} %bitcast.115, f32[]{:T(128)} %broadcast.873), dimensions={1}, to_apply=%bitcast.103.reduce_sub_computation | reduce | bytes 172036
  86.5 4.3 reshape.854
  90.8 9.0 %all-to-all-start.1 = ((f32[64,1,336]{2,1,0:T(1,128)}), f32[64,1,336]{2,1,0:T(1,128)S(1)}, u32[]{:S(2)}, u32[]{:S(2)}) async-start(f32[64,1,336]{2,1,0:T(1,128)} %reshape.854), calls=%async_computation.1 | async-start | bytes 196608 | tf_op jit(solution)/shard_map/all_to_all | solution.py:134
  99.9 11.4 %all-to-all-done.1 = f32[64,1,336]{2,1,0:T(1,128)S(1)} async-done(((f32[64,1,336]{2,1,0:T(1,128)}), f32[64,1,336]{2,1,0:T(1,128)S(1)}, u32[]{:S(2)}, u32[]{:S(2)}) %all-to-all-start.1) | async-done | bytes 86048 | tf_op jit(solution)/shard_map/all_to_all | solution.py:134
  111.3 0.9 reduce.11
  112.1 6.9 reshape.855
  119.0 7.1 %copy.68 = f32[3,1,7168]{2,0,1:T(4,128)S(1)} copy(f32[3,1,7168]{0,1,2:T(1,128)} %bitcast.114) | data formatting | bytes 172032 | tf_op jit(solution)/shard_map/all_to_all | solution.py:134
  126.1 0.7 reshape.831
  127.5 19.9 %fusion = f32[28,3585,3,2]{1,3,2,0:T(2,128)} fusion(bf16[28,32,3585]{2,1,0:T(8,128)(2,1)} %param.11, f32[28,3585,2,2]{1,2,3,0:T(2,128)S(1)} %copy.95, bf16[3,1,32,2,2,28]{2,4,3,1,0,5:T(2,128)(2,1)S(1)} %get-tuple-element.17, bf16[3,1,32,2,2,28]{2,4,3,1,0,5:T(2,128)(2,1)S(1)} %get-tuple-element.16), kind=kOutput, calls=%fused_computation.1 | convolution fusion | flops 158485664 | bytes 10482528 | tf_op jit(solution)/shard_map/ijk,fqjrai->afqrik/dot_general | solution.py:140
  147.4 3.4 copy.104
  150.8 1.8 add_convert_fusion.1
  152.6 1.7 add_convert_fusion
  154.3 1.0 fusion.20
  155.3 84.5 %all-gather.3.cloned.1.call-done = f32[12,2,28,3585]{3,1,2,0:T(2,128)} async-done(((f32[3,2,28,3585]{3,1,2,0:T(2,128)}), f32[12,2,28,3585]{3,1,2,0:T(2,128)}) %all-gather.3.cloned.1.call-update) | async-done | bytes 9636496 | tf_op jit(solution)/shard_map/all_gather | solution.py:156
  239.9 13.5 %reduce_sum.9 = f32[3,2,28,3585]{3,1,2,0:T(2,128)S(1)} reduce(f32[4,3,2,28,3585]{4,2,3,1,0:T(2,128)} %bitcast.116, f32[]{:T(128)} %constant.118.clone.1), dimensions={0}, to_apply=%region_0.1 | reduce | flops 1806840 | bytes 12045604 | tf_op jit(solution)/shard_map/reduce_sum | solution.py:156
  253.4 2.5 fusion.182
  255.9 0.8 add_convert_fusion.2
  256.7 3.2 broadcast_multiply_fusion
  259.9 7.7 %fusion.8 = f32[2,2,32,2,2,28]{2,3,0,1,4,5:T(2,128)S(1)} fusion(bf16[28,32,3585]{2,1,0:T(8,128)(2,1)} %param.11, bf16[2,28,3585]{2,0,1:T(2,128)(2,1)S(1)} %copy-done.3, bf16[2,2,2,28,3585]{4,2,1,0,3:T(2,128)(2,1)S(1)} %broadcast_multiply_fusion), kind=kOutput, calls=%fused_computation.20 | convolution fusion | flops 109213440 | bytes 8489264 | tf_op jit(solution)/shard_map/ijk,aqfrik->fqjrai/dot_general | solution.py:164
  267.8 0.3 copy.91
  268.1 0.9 reshape.849
  269.0 13.1 %all-to-all-start.2 = ((f32[2,64,112]{2,0,1:T(2,128)}), f32[2,64,112]{2,0,1:T(2,128)S(1)}, u32[]{:S(2)}, u32[]{:S(2)}) async-start(f32[2,64,112]{2,0,1:T(2,128)} %reshape.849), calls=%async_computation.2 | async-start | bytes 131072 | tf_op jit(solution)/shard_map/all_to_all | solution.py:173
  282.0 11.1 %all-to-all-done.2 = f32[2,64,112]{2,0,1:T(2,128)S(1)} async-done(((f32[2,64,112]{2,0,1:T(2,128)}), f32[2,64,112]{2,0,1:T(2,128)S(1)}, u32[]{:S(2)}, u32[]{:S(2)}) %all-to-all-start.2) | async-done | bytes 57376 | tf_op jit(solution)/shard_map/all_to_all | solution.py:173
  293.8 1.3 rev.11
  295.3 0.4 fusion.70
  295.7 0.4 fusion.72
  296.2 0.4 convolution_add_fusion
  296.6 0.4 convolution_subtract_fusion.1
  297.0 0.5 fusion.36
  297.5 0.5 fusion.13
  298.0 0.3 reshape.836
  298.3 11.8 %copy.77 = f32[2,1,16000]{0,1,2:T(1,128)} copy(f32[2,1,16000]{2,0,1:T(2,128)S(1)} %reshape.836) | data formatting | bytes 256000 | tf_op jit(solution)/shard_map/reshape | solution.py:111
  310.1 72.8 %reduce.12 = f32[16000,2]{1,0:T(8,128)} reduce(f32[16000,1,2]{2,1,0:T(1,128)} %bitcast.113, f32[]{:T(128)} %broadcast.873), dimensions={1}, to_apply=%bitcast.105.reduce_sub_computation | reduce | bytes 256004
  382.9 6.7 reshape.856
  389.6 17.2 %all_to_all.16 = f32[64,1,500]{2,1,0:T(1,128)S(1)} all-to-all(f32[64,1,500]{2,1,0:T(1,128)S(1)} %reshape.856), channel_id=1, replica_groups=mesh['lon'=64,'lat'=4] {'lon'}, dimensions={0} | all-to-all | bytes 256000 | tf_op jit(solution)/shard_map/all_to_all | solution.py:178
  406.8 1.0 reduce.13
  407.8 10.4 %reshape.857 = f32[16000,1,2]{2,1,0:T(1,128)} reshape(f32[64,500]{1,0:T(8,128)S(1)} %reduce.13) | data formatting | bytes 256000
  418.2 263.2 %slice_reduce_fusion = (f32[16000]{0:T(1024)S(1)}, f32[16000]{0:T(1024)S(1)}) fusion(f32[2,1,16000]{0,1,2:T(1,128)} %bitcast.112), kind=kLoop, calls=%fused_computation.2 | loop fusion | bytes 256000 | tf_op jit(solution)/shard_map/slice | solution.py:179
  681.4 0.8 squeeze.34
  682.3 0.8 squeeze.16
  (51 shorter events, 3.4 us)
Async XLA Ops:
  10.0 28.4 %all-to-all-start = ((f32[3,64,250]{2,0,1:T(4,128)}), f32[3,64,250]{2,0,1:T(4,128)S(1)}, u32[]{:S(2)}, u32[]{:S(2)}) async-start(f32[3,64,250]{2,0,1:T(4,128)} %pad_maximum_fusion.1), calls=%async_computation | async-start | bytes 524288 | tf_op jit(solution)/shard_map/all_to_all | solution.py:130
  86.5 13.3 %copy-start.4 = (f32[32]{0:T(128)S(1)}, f32[32]{0:T(128)}, u32[]{:S(2)}) copy-start(f32[32]{0:T(128)} %param.10) | copy-start | bytes 388
  90.8 20.4 %all-to-all-start.1 = ((f32[64,1,336]{2,1,0:T(1,128)}), f32[64,1,336]{2,1,0:T(1,128)S(1)}, u32[]{:S(2)}, u32[]{:S(2)}) async-start(f32[64,1,336]{2,1,0:T(1,128)} %reshape.854), calls=%async_computation.1 | async-start | bytes 196608 | tf_op jit(solution)/shard_map/all_to_all | solution.py:134
  99.8 140.1 %all-gather.3.cloned.1.call-start = ((), (), s32[]{:S(2)}) async-start(), calls=%async_computation.4 | async-start | bytes 12472320 | tf_op jit(solution)/shard_map/all_gather | solution.py:156
  147.4 3.4 copy-start.1
  147.4 5.2 copy-start
  253.4 3.3 copy-start.2
  255.9 4.0 copy-start.3
  269.0 24.2 %all-to-all-start.2 = ((f32[2,64,112]{2,0,1:T(2,128)}), f32[2,64,112]{2,0,1:T(2,128)S(1)}, u32[]{:S(2)}, u32[]{:S(2)}) async-start(f32[2,64,112]{2,0,1:T(2,128)} %reshape.849), calls=%async_computation.2 | async-start | bytes 131072 | tf_op jit(solution)/shard_map/all_to_all | solution.py:173
Sparse Core Ops, SparseCore 0:
  150.9 88.9 all-gather.2
